TPU v7x, 32 devices: a whole 2x2x4 slice. The times are simulated.
32 devices in a mesh: frame: 4 (over z), space: 8 (over y, x, core).
Axes of the slice: x: 2, y: 2, z: 4, core: 2. Of those that a mesh axis runs over, the one named last changes fastest.
Arguments:
- latents: bfloat16 [2, 4, 512, 3072], P(None, 'frame', 'space'), may hold values from -6 to 6
- target: bfloat16 [2, 4, 512, 3072], P(None, 'frame', 'space'), may hold values from -6 to 6
- timesteps: int32 [2], replicated, may hold values from 0 to 999
- valid: int32 [2, 2], replicated, may hold values from 1 to 16, as said below
- tile_mask: int32 [2, 16, 16], replicated, may hold values from 0 to 1, as said below
- w_mod: bfloat16 [256, 18432], replicated, may hold values from -0.5 to 0.5
- w_sqkv: bfloat16 [3, 3072, 2048], P(None, None, 'space'), may hold values from -0.109375 to 0.109375
- w_sout: bfloat16 [2048, 3072], P('space'), may hold values from -0.125 to 0.125
- w_tqkv: bfloat16 [3, 3072, 2048], P(None, None, 'frame'), may hold values from -0.109375 to 0.109375
- w_tout: bfloat16 [2048, 3072], P('frame'), may hold values from -0.125 to 0.125
Outputs:
- mixed: bfloat16 [2, 4, 512, 3072], P(None, 'frame', 'space')
- loss: float32 [], replicated
Inputs may be any that keep to these rules, and one draw needn't show every extreme that they name: Each video's valid frame count is 1 to 4 and valid tile count 1 to 16; video 0 is whole. `tile_mask`: entries are 0 or 1, with ones on the diagonal of every video's mask.
All inputs are finite; a program needn't handle non-finite values.
Results may differ from a plain program's by a relative error of at most 0.017.
Values may be sent and summed in bfloat16 or wider, within the bound.
A program may use at most 128 MiB of HBM per device.

v0:
```python
import math
import jax
import jax.numpy as jnp
from jax import lax
from jax.sharding import PartitionSpec as P

HEAD_DIM = 128
FREQ = 256
TILE = 32


def layer_norm(values):
    mean = jnp.mean(values, -1, keepdims=True)
    centred = values - mean
    var = jnp.mean(centred * centred, -1, keepdims=True)
    return centred * lax.rsqrt(var + 1e-06)


def time_embed(timesteps):
    half = FREQ // 2
    freqs = jnp.exp(-math.log(10000.0) * jnp.arange(half, dtype=jnp.float32) / half)
    angles = timesteps.astype(jnp.float32)[:, None] * freqs[None, :]
    return jnp.concatenate([jnp.cos(angles), jnp.sin(angles)], -1).astype(jnp.bfloat16)


def modulate(values, shift, scale):
    return (
        layer_norm(values.astype(jnp.float32)) * (1.0 + scale[:, None, None, :])
        + shift[:, None, None, :]
    ).astype(jnp.bfloat16)


def frame_attention(qkv, count, tiles, heads):
    length = qkv.shape[0]
    cols = heads * HEAD_DIM
    scale = 1.0 / math.sqrt(HEAD_DIM)
    query = jnp.transpose(qkv[:, :cols].reshape(length, heads, HEAD_DIM), (1, 0, 2))
    keys = jnp.transpose(qkv[:, cols : 2 * cols].reshape(length, heads, HEAD_DIM), (1, 0, 2))
    values = jnp.transpose(qkv[:, 2 * cols :].reshape(length, heads, HEAD_DIM), (1, 0, 2))
    tile_ids = jnp.arange(length, dtype=jnp.int32) // TILE
    expanded = jnp.repeat(jnp.repeat(tiles, TILE, axis=0), TILE, axis=1)
    allowed = (expanded == 1) & (tile_ids[None, :] < count) | (
        tile_ids[:, None] == tile_ids[None, :]
    )

    def one_head(parts):
        q_head, k_head, v_head = parts
        scores = (
            lax.dot_general(
                q_head, k_head, (((1,), (1,)), ((), ())), preferred_element_type=jnp.float32
            )
            * scale
        )
        scores = jnp.where(allowed, scores, -1e30)
        top = jnp.max(scores, -1, keepdims=True)
        weights = jnp.exp(scores - top)
        probs = (weights / jnp.sum(weights, -1, keepdims=True)).astype(jnp.bfloat16)
        return jnp.dot(probs, v_head, preferred_element_type=jnp.float32).astype(jnp.bfloat16)

    outs = lax.map(one_head, (query, keys, values))
    return jnp.transpose(outs, (1, 0, 2)).reshape(length, cols)


def temporal_attention(qkv, count, heads):
    frames, places = (qkv.shape[0], qkv.shape[1])
    cols = heads * HEAD_DIM
    scale = 1.0 / math.sqrt(HEAD_DIM)
    query = qkv[..., :cols].reshape(frames, places, heads, HEAD_DIM)
    keys = qkv[..., cols : 2 * cols].reshape(frames, places, heads, HEAD_DIM)
    values = qkv[..., 2 * cols :].reshape(frames, places, heads, HEAD_DIM)
    scores = jnp.einsum("fphd,gphd->phfg", query, keys, preferred_element_type=jnp.float32) * scale
    frame_ids = jnp.arange(frames, dtype=jnp.int32)
    allowed = (frame_ids[None, :] < count) | (frame_ids[:, None] == frame_ids[None, :])
    scores = jnp.where(allowed, scores, -1e30)
    top = jnp.max(scores, -1, keepdims=True)
    weights = jnp.exp(scores - top)
    probs = (weights / jnp.sum(weights, -1, keepdims=True)).astype(jnp.bfloat16)
    outs = jnp.einsum("phfg,gphd->fphd", probs, values, preferred_element_type=jnp.float32).astype(
        jnp.bfloat16
    )
    return outs.reshape(frames, places, cols)


def group_project(attended, w_out, groups):
    rows = attended.shape[0]
    width = w_out.shape[1]
    parts = attended.reshape(rows, groups, -1)
    weights = w_out.reshape(groups, -1, width)
    terms = jnp.einsum("rgc,gcd->rgd", parts, weights, preferred_element_type=jnp.float32).astype(
        jnp.bfloat16
    )
    return jnp.sum(terms.astype(jnp.float32), axis=1)


def shards(latents, target, timesteps, valid, tile_mask, w_mod, w_sqkv, w_sout, w_tqkv, w_tout):
    videos, frames_dev, span_dev, width = latents.shape
    space_count = lax.axis_size("space")
    frame_count = lax.axis_size("frame")
    embed = time_embed(timesteps)
    mod = jnp.dot(embed, w_mod, preferred_element_type=jnp.float32)
    shift_one, scale_one, gate_one, shift_two, scale_two, gate_two = jnp.split(mod, 6, axis=1)
    h_one = modulate(latents, shift_one, scale_one)
    spatial_heads = w_sqkv.shape[2] // HEAD_DIM
    w_flat = jnp.concatenate([w_sqkv[0], w_sqkv[1], w_sqkv[2]], axis=1)
    qkv_space = jnp.dot(
        lax.all_gather(h_one, "space", axis=2, tiled=True),
        w_flat,
        preferred_element_type=jnp.float32,
    ).astype(jnp.bfloat16)
    span = qkv_space.shape[2]
    frames_flat = qkv_space.reshape(videos * frames_dev, span, -1)
    tile_counts = jnp.repeat(valid[:, 1], frames_dev)
    tiles = jnp.repeat(tile_mask, frames_dev, axis=0)

    def per_frame(parts):
        frame_qkv, count, tiles_one = parts
        return frame_attention(frame_qkv, count, tiles_one, spatial_heads)

    spatial_att = lax.map(per_frame, (frames_flat, tile_counts, tiles)).reshape(
        videos, frames_dev, span, -1
    )
    spatial_att = jnp.transpose(spatial_att, (2, 0, 1, 3))
    w_sall = lax.all_gather(w_sout, "space", axis=0, tiled=True)
    own_rows = lax.all_to_all(spatial_att, "space", split_axis=0, concat_axis=3, tiled=True)
    spatial = group_project(
        own_rows.reshape(span_dev * videos * frames_dev, -1), w_sall, space_count
    )
    spatial = spatial.reshape(span_dev, videos, frames_dev, width)
    spatial = jnp.transpose(spatial, (1, 2, 0, 3))
    x_one = (latents.astype(jnp.float32) + gate_one[:, None, None, :] * spatial).astype(
        jnp.bfloat16
    )
    h_two = modulate(x_one, shift_two, scale_two)
    temporal_heads = w_tqkv.shape[2] // HEAD_DIM
    w_tflat = jnp.concatenate([w_tqkv[0], w_tqkv[1], w_tqkv[2]], axis=1)
    qkv_frame = jnp.dot(
        lax.all_gather(h_two, "frame", axis=1, tiled=True),
        w_tflat,
        preferred_element_type=jnp.float32,
    ).astype(jnp.bfloat16)

    def per_video(parts):
        video_qkv, count = parts
        return temporal_attention(video_qkv, count, temporal_heads)

    temporal_att = lax.map(per_video, (qkv_frame, valid[:, 0]))
    temporal_att = jnp.transpose(temporal_att, (1, 0, 2, 3))
    w_tall = lax.all_gather(w_tout, "frame", axis=0, tiled=True)
    own_frames = lax.all_to_all(temporal_att, "frame", split_axis=0, concat_axis=3, tiled=True)
    temporal = group_project(
        own_frames.reshape(frames_dev * videos * span_dev, -1), w_tall, frame_count
    )
    temporal = temporal.reshape(frames_dev, videos, span_dev, width)
    temporal = jnp.transpose(temporal, (1, 0, 2, 3))
    mixed = (x_one.astype(jnp.float32) + gate_two[:, None, None, :] * temporal).astype(jnp.bfloat16)
    diff = mixed.astype(jnp.float32) - target.astype(jnp.float32)
    squares = jnp.mean(diff * diff, -1)
    frame_ids = lax.axis_index("frame") * frames_dev + jnp.arange(frames_dev, dtype=jnp.int32)
    tile_ids = (lax.axis_index("space") * span_dev + jnp.arange(span_dev, dtype=jnp.int32)) // TILE
    mask = (frame_ids[None, :, None] < valid[:, 0][:, None, None]) & (
        tile_ids[None, None, :] < valid[:, 1][:, None, None]
    )
    local_total = jnp.sum(jnp.where(mask, squares, 0.0))
    total = lax.psum(local_total, ("frame", "space"))
    count = jnp.sum(valid[:, 0] * valid[:, 1]).astype(jnp.float32) * TILE
    return (mixed, total / count)


def solution(mesh):
    return jax.shard_map(
        shards,
        mesh=mesh,
        in_specs=(
            P(None, "frame", "space", None),
            P(None, "frame", "space", None),
            P(),
            P(),
            P(),
            P(),
            P(None, None, "space"),
            P("space", None),
            P(None, None, "frame"),
            P("frame", None),
        ),
        out_specs=(P(None, "frame", "space", None), P()),
        check_vma=False,
    )
```

profile of v0, /device:TPU:12, one launch (start us, length us, event | category | flops | bytes accessed | tf_op | source)
XLA Modules:
  0.0 503.2 jit_solution(8383597021539726154)
XLA Ops:
  7.2 0.7 convert_element_type.72
  8.0 5.1 %fusion.68 = f32[2,18432]{1,0:T(2,128)S(1)} fusion(bf16[256,18432]{1,0:T(8,128)(2,1)} %param.21, bf16[2,128]{1,0:T(2,128)(2,1)S(1)} %get-tuple-element.260, bf16[2,128]{1,0:T(2,128)(2,1)S(1)} %get-tuple-element.259), kind=kOutput, calls=%fused_computation.113 | convolution fusion | flops 18876416 | bytes 9585664 | tf_op jit(solution)/shard_map/dot_general | solution.py:100
  13.7 1.3 fusion.62
  15.1 0.7 all-gather.7.cloned.1.call-update
  16.0 4.4 slice_bitcast_fusion.5
  20.4 41.2 %all-gather.5.cloned.1.call-done = bf16[2,1,512,3072]{3,2,0,1:T(8,128)(2,1)} async-done(((bf16[2,1,64,3072]{3,2,0,1:T(8,128)(2,1)}), bf16[2,1,512,3072]{3,2,0,1:T(8,128)(2,1)}) %all-gather.5.cloned.1.call-update) | async-done | bytes 6291472 | tf_op jit(solution)/shard_map/all_gather | solution.py:106
  61.6 9.9 %fusion.52 = bf16[2,512,768]{2,1,0:T(8,128)(2,1)} fusion(bf16[3072,256]{1,0:T(8,128)(2,1)} %get-tuple-element.251, bf16[3072,256]{1,0:T(8,128)(2,1)} %get-tuple-element.252, bf16[3072,256]{1,0:T(8,128)(2,1)S(1)} %get-tuple-element.250, bf16[2,1,512,3072]{3,2,0,1:T(8,128)(2,1)} %all-gather.5.cloned.1.call-done), kind=kOutput, calls=%fused_computation.84 | convolution fusion | flops 4846780416 | bytes 12582912 | tf_op jit(solution)/shard_map/dot_general | solution.py:105
  71.4 12.7 %while.43 = (s32[]{:T(128)}, bf16[2,512,256]{2,1,0:T(8,128)(2,1)S(1)}, bf16[2,512,768]{2,1,0:T(8,128)(2,1)}, s32[2,16,16]{2,1,0:T(8,128)S(1)}, s32[2]{0:T(128)S(1)}, /*index=5*/s32[]{:T(128)}, s32[]{:T(128)}, s32[]{:T(128)}) while((s32[]{:T(128)}, bf16[2,512,256]{2,1,0:T(8,128)(2,1)S(1)}, bf16[2,512,768]{2,1,0:T(8,128)(2,1)}, ...), condition=%wide.region_7.8_spmd, body=%wide.region_2.7_spmd.sunk | while | flops 137174784 | bytes 10541854 | solution.py:119
  71.4 1.3 constant_dynamic-slice_fusion.4
  73.4 0.6 dynamic_slice.70
  74.0 0.7 broadcast_compare_fusion.3
  74.7 2.7 while.45
  76.9 0.4 fusion.117
  77.9 1.2 constant_dynamic-slice_fusion.4
  79.7 0.6 dynamic_slice.70
  80.3 0.7 broadcast_compare_fusion.3
  81.0 2.7 while.45
  81.9 0.4 fusion.117
  83.2 0.4 fusion.117
  84.2 0.5 copy.99
  84.7 12.6 %all_to_all.30 = bf16[512,2,1,256]{3,1,2,0:T(2,128)(2,1)S(1)} all-to-all(bf16[512,2,1,256]{3,1,2,0:T(2,128)(2,1)S(1)} %bitcast.158), channel_id=1, replica_groups=mesh['frame'=4,'space'=8] {'space'}, dimensions={0} | all-to-all | bytes 1048576 | tf_op jit(solution)/shard_map/all_to_all | solution.py:124
  97.5 42.3 %all-gather.7.cloned.1.call-done = bf16[2048,3072]{1,0:T(8,128)(2,1)} async-done(((bf16[256,3072]{1,0:T(8,128)(2,1)}), bf16[2048,3072]{1,0:T(8,128)(2,1)}) %all-gather.7.cloned.1.call-update) | async-done | bytes 12582928 | tf_op jit(solution)/shard_map/all_gather | solution.py:123
  139.8 7.7 %convert_reduce_fusion = f32[128,3072]{1,0:T(8,128)} fusion(bf16[128,8,256]{2,0,1:T(8,128)(2,1)S(1)} %reshape_reshape.6, bf16[8,256,3072]{2,1,0:T(8,128)(2,1)} %bitcast.152), kind=kOutput, calls=%fused_computation.53 | convolution fusion | flops 1619656704 | bytes 14680064 | tf_op jit(solution)/shard_map/rgc,gcd->rgd/dot_general | solution.py:89
  147.5 2.2 reshape.315
  149.7 0.7 convert_reduce_fusion.2
  150.8 1.3 fusion.58
  152.2 0.5 all-gather.11.cloned.1.call-update
  152.7 6.7 %slice_bitcast_fusion.2 = (bf16[3072,512]{1,0:T(8,128)(2,1)}, bf16[3072,512]{1,0:T(8,128)(2,1)}, bf16[3072,512]{1,0:T(8,128)(2,1)}) fusion(bf16[3,3072,512]{2,1,0:T(8,128)(2,1)} %param.24), kind=kLoop, calls=%fused_computation.72 | loop fusion | bytes 18874368 | tf_op jit(solution)/shard_map/squeeze | solution.py:135
  159.5 54.6 %all-gather.9.cloned.1.call-done = bf16[2,4,64,3072]{3,2,0,1:T(8,128)(2,1)} async-done(((bf16[2,1,64,3072]{3,2,0,1:T(8,128)(2,1)}), bf16[2,4,64,3072]{3,2,0,1:T(8,128)(2,1)}) %all-gather.9.cloned.1.call-update) | async-done | bytes 3145744 | tf_op jit(solution)/shard_map/all_gather | solution.py:137
  214.0 9.7 %fusion.45 = bf16[2,4,64,1536]{3,2,1,0:T(8,128)(2,1)S(1)} fusion(bf16[3072,512]{1,0:T(8,128)(2,1)} %get-tuple-element.248, bf16[3072,512]{1,0:T(8,128)(2,1)} %get-tuple-element.249, bf16[3072,512]{1,0:T(8,128)(2,1)} %get-tuple-element.247, bf16[2,4,64,3072]{3,2,0,1:T(8,128)(2,1)} %all-gather.9.cloned.1.call-done), kind=kOutput, calls=%fused_computation.73 | convolution fusion | flops 4860936192 | bytes 14155776 | tf_op jit(solution)/shard_map/dot_general | solution.py:136
  223.7 11.9 %while.44 = (s32[]{:T(128)}, bf16[2,4,64,512]{3,2,0,1:T(8,128)(2,1)}, bf16[2,4,64,1536]{3,2,1,0:T(8,128)(2,1)S(1)}, s32[2]{0:T(128)S(1)}, s32[]{:T(128)}) while((s32[]{:T(128)}, bf16[2,4,64,512]{3,2,0,1:T(8,128)(2,1)}, bf16[2,4,64,1536]{3,2,1,0:T(8,128)(2,1)S(1)}, s32[2]{0:T(128)S(1)}, s32[]{:T(128)}) %tuple.106), condition=%wide.region_14.15_spmd, body=%wide.region_11.14_spmd.sunk | while | flops 2252841 | bytes 7479929 | solution.py:146
  224.0 0.8 reshape.325
  224.7 1.4 fusion.109
  226.5 0.6 dynamic_slice.72
  227.1 0.7 iota_compare_fusion.3
  228.9 0.7 bitcast_dynamic-update-slice_fusion.2
  229.9 0.8 reshape.325
  230.7 1.4 fusion.109
  232.4 0.6 dynamic_slice.72
  233.0 0.7 iota_compare_fusion.3
  234.8 0.7 bitcast_dynamic-update-slice_fusion.2
  235.6 6.2 %all-to-all-start.1 = ((bf16[4,2,64,512]{3,2,1,0:T(8,128)(2,1)}), bf16[4,2,64,512]{3,2,1,0:T(8,128)(2,1)S(1)}, u32[]{:S(2)}, u32[]{:S(2)}) async-start(bf16[4,2,64,512]{3,2,1,0:T(8,128)(2,1)} %bitcast.161), calls=%async_computation.1 | async-start | bytes 1048576 | tf_op jit(solution)/shard_map/all_to_all | solution.py:149
  241.8 0.6 multiply_reduce_fusion.1
  243.1 198.7 %all-gather.11.cloned.1.call-done = bf16[2048,3072]{1,0:T(8,128)(2,1)} async-done(((bf16[512,3072]{1,0:T(8,128)(2,1)}), bf16[2048,3072]{1,0:T(8,128)(2,1)}) %all-gather.11.cloned.1.call-update) | async-done | bytes 12582928 | tf_op jit(solution)/shard_map/all_gather | solution.py:148
  441.8 6.6 %convert_reduce_fusion.1 = f32[128,3072]{1,0:T(8,128)S(1)} fusion(bf16[128,4,512]{2,0,1:T(8,128)(2,1)S(1)} %bitcast.157, bf16[4,512,3072]{2,1,0:T(8,128)(2,1)} %bitcast.153), kind=kOutput, calls=%fused_computation.62 | convolution fusion | flops 1614938112 | bytes 14680064 | tf_op jit(solution)/shard_map/rgc,gcd->rgd/dot_general | solution.py:89
  448.4 1.4 multiply_reduce_fusion
  449.8 0.7 fusion.67
  450.5 44.4 %psum.7 = f32[]{:T(128)} all-reduce(f32[]{:T(128)} %fusion.67), channel_id=1, replica_groups=mesh['frame'=4,'space'=8] {'frame','space'}, use_global_device_ids=true, to_apply=%region_18.19 | all-reduce | flops 1 | bytes 8 | tf_op jit(solution)/shard_map/psum | solution.py:164
  (92 shorter events, 11.2 us)
Async XLA Ops:
  7.2 54.4 %all-gather.5.cloned.1.call-start = ((), (), s32[]{:S(2)}) async-start(), calls=%async_computation.2 | async-start | bytes 7077888 | tf_op jit(solution)/shard_map/all_gather | solution.py:106
  8.0 5.1 %copy-start = (bf16[2,1,64,3072]{3,2,1,0:T(8,128)(2,1)S(1)}, bf16[2,1,64,3072]{3,2,1,0:T(8,128)(2,1)}, u32[]{:S(2)}) copy-start(bf16[2,1,64,3072]{3,2,1,0:T(8,128)(2,1)} %param.16) | copy-start | bytes 2359300
  15.0 0.8 copy-start.3
  15.0 124.8 %all-gather.7.cloned.1.call-start = ((), (), s32[]{:S(2)}) async-start(), calls=%async_computation.3 | async-start | bytes 14155776 | tf_op jit(solution)/shard_map/all_gather | solution.py:123
  15.8 198.3 %all-gather.9.cloned.1.call-start = ((), (), s32[]{:S(2)}) async-start(), calls=%async_computation.4 | async-start | bytes 3932160 | tf_op jit(solution)/shard_map/all_gather | solution.py:137
  61.6 9.9 %copy-start.2 = (s32[2,16,16]{2,1,0:T(8,128)S(1)}, s32[2,16,16]{2,1,0:T(8,128)}, u32[]{:S(2)}) copy-start(s32[2,16,16]{2,1,0:T(8,128)} %param.20) | copy-start | bytes 6148
  152.1 289.7 %all-gather.11.cloned.1.call-start = ((), (), s32[]{:S(2)}) async-start(), calls=%async_computation.5 | async-start | bytes 15728640 | tf_op jit(solution)/shard_map/all_gather | solution.py:148
  235.6 206.2 %all-to-all-start.1 = ((bf16[4,2,64,512]{3,2,1,0:T(8,128)(2,1)}), bf16[4,2,64,512]{3,2,1,0:T(8,128)(2,1)S(1)}, u32[]{:S(2)}, u32[]{:S(2)}) async-start(bf16[4,2,64,512]{3,2,1,0:T(8,128)(2,1)} %bitcast.161), calls=%async_computation.1 | async-start | bytes 1048576 | tf_op jit(solution)/shard_map/all_to_all | solution.py:149
  441.8 6.6 %copy-start.1 = (bf16[2,1,64,3072]{3,2,1,0:T(8,128)(2,1)S(1)}, bf16[2,1,64,3072]{3,2,1,0:T(8,128)(2,1)}, u32[]{:S(2)}) copy-start(bf16[2,1,64,3072]{3,2,1,0:T(8,128)(2,1)} %param.17) | copy-start | bytes 2359300
Sparse Core Ops, SparseCore 0:
  15.1 46.3 all-gather.4
  63.5 76.3 all-gather.6
  152.2 61.7 all-gather.8
  215.5 226.2 all-gather.10
where the time goes:
time: 504 us; the launch traced here: 503 us
  waiting for transfers between devices  338 us (67%)
  blocking collectives  57 us (11%)
  matrix products  45.9 us (9%)
  local copies, waits for them, and re-layouts  26.5 us (5%)
  between operations  16.3 us (3%)
  other arithmetic  12.6 us (2%)
  starting transfers between devices  6.4 us (1%)
    all_gather x1, waiting for transfers between devices, shards(): w_tall = lax.all_gather(w_tout, 'frame', axis=0, tiled=True)  199 us
    all_gather x1, waiting for transfers between devices, shards(): lax.all_gather(h_two, 'frame', axis=1, tiled=True)  54.6 us
    psum x1, blocking collectives, shards(): total = lax.psum(local_total, ('frame', 'space'))  44.4 us
    all_gather x1, waiting for transfers between devices, shards(): w_sall = lax.all_gather(w_sout, 'space', axis=0, tiled=True)  42.3 us
    all_gather x1, waiting for transfers between devices, shards(): lax.all_gather(h_one, 'space', axis=2, tiled=True)  41.2 us
    dot_general x2, matrix products, group_project(): jnp.einsum('rgc,gcd->rgd', parts, weights, preferred_element_type=jnp.flo...  14.3 us
    all_to_all x1, blocking collectives, shards(): lax.all_to_all(spatial_att, 'space', split_axis=0, concat_axis=3, tiled=T...  12.6 us
  transfers between devices with their start and end apart: 5, of which 4 were waited for; matrix products, arithmetic and copies ran while one was open for 11% of the time, Pallas kernels for 0%

commit v1 on v0

--- a/solution.py
+++ b/solution.py
@@ -121,7 +121,15 @@
     )
     spatial_att = jnp.transpose(spatial_att, (2, 0, 1, 3))
     w_sall = lax.all_gather(w_sout, "space", axis=0, tiled=True)
-    own_rows = lax.all_to_all(spatial_att, "space", split_axis=0, concat_axis=3, tiled=True)
+    own_rows = jnp.concatenate(
+        lax.all_to_all(
+            jnp.stack(jnp.split(spatial_att, lax.axis_size("space"), axis=0)),
+            axis_name="space",
+            split_axis=0,
+            concat_axis=0,
+        ),
+        axis=3,
+    )
     spatial = group_project(
         own_rows.reshape(span_dev * videos * frames_dev, -1), w_sall, space_count
     )

time: 504 us -> 504 us (level)
  no operation moved by 1% of the time
where the time goes in v1:
time: 504 us
  waiting for transfers between devices  338 us (67%)
  blocking collectives  57.4 us (11%)
  matrix products  45.9 us (9%)
  local copies, waits for them, and re-layouts  26.6 us (5%)
  between operations  16.4 us (3%)
  other arithmetic  12.6 us (2%)
  starting transfers between devices  6.4 us (1%)
    all_gather x1, waiting for transfers between devices, shards(): w_tall = lax.all_gather(w_tout, 'frame', axis=0, tiled=True)  199 us
    all_gather x1, waiting for transfers between devices, shards(): lax.all_gather(h_two, 'frame', axis=1, tiled=True)  54.6 us
    psum x1, blocking collectives, shards(): total = lax.psum(local_total, ('frame', 'space'))  44.4 us
    all_gather x1, waiting for transfers between devices, shards(): w_sall = lax.all_gather(w_sout, 'space', axis=0, tiled=True)  42.2 us
    all_gather x1, waiting for transfers between devices, shards(): lax.all_gather(h_one, 'space', axis=2, tiled=True)  41.2 us
    dot_general x2, matrix products, group_project(): jnp.einsum('rgc,gcd->rgd', parts, weights, preferred_element_type=jnp.flo...  14.3 us
    all_to_all x1, blocking collectives, shards(): lax.all_to_all(jnp.stack(jnp.split(spatial_att, lax.axis_size('space'), a...  13 us
  transfers between devices with their start and end apart: 5, of which 4 were waited for; matrix products, arithmetic and copies ran while one was open for 11% of the time, Pallas kernels for 0%

profile of v1, /device:TPU:12, one launch (start us, length us, event | category | flops | bytes accessed | tf_op | source)
XLA Modules:
  0.0 503.6 jit_solution(8163191770682136042)
XLA Ops:
  7.2 0.7 convert_element_type.72
  8.0 5.1 %fusion.76 = f32[2,18432]{1,0:T(2,128)S(1)} fusion(bf16[256,18432]{1,0:T(8,128)(2,1)} %param.21, bf16[2,128]{1,0:T(2,128)(2,1)S(1)} %get-tuple-element.260, bf16[2,128]{1,0:T(2,128)(2,1)S(1)} %get-tuple-element.259), kind=kOutput, calls=%fused_computation.128 | convolution fusion | flops 18876416 | bytes 9585664 | tf_op jit(solution)/shard_map/dot_general | solution.py:100
  13.7 1.3 fusion.62
  15.1 0.7 all-gather.7.cloned.1.call-update
  16.0 4.4 slice_bitcast_fusion.5
  20.4 41.2 %all-gather.5.cloned.1.call-done = bf16[2,1,512,3072]{3,2,0,1:T(8,128)(2,1)} async-done(((bf16[2,1,64,3072]{3,2,0,1:T(8,128)(2,1)}), bf16[2,1,512,3072]{3,2,0,1:T(8,128)(2,1)}) %all-gather.5.cloned.1.call-update) | async-done | bytes 6291472 | tf_op jit(solution)/shard_map/all_gather | solution.py:106
  61.6 9.9 %fusion.52 = bf16[2,512,768]{2,1,0:T(8,128)(2,1)} fusion(bf16[3072,256]{1,0:T(8,128)(2,1)} %get-tuple-element.251, bf16[3072,256]{1,0:T(8,128)(2,1)} %get-tuple-element.252, bf16[3072,256]{1,0:T(8,128)(2,1)S(1)} %get-tuple-element.250, bf16[2,1,512,3072]{3,2,0,1:T(8,128)(2,1)} %all-gather.5.cloned.1.call-done), kind=kOutput, calls=%fused_computation.84 | convolution fusion | flops 4846780416 | bytes 12582912 | tf_op jit(solution)/shard_map/dot_general | solution.py:105
  71.4 12.7 %while.43 = (s32[]{:T(128)}, bf16[2,512,256]{2,1,0:T(8,128)(2,1)S(1)}, bf16[2,512,768]{2,1,0:T(8,128)(2,1)}, s32[2,16,16]{2,1,0:T(8,128)S(1)}, s32[2]{0:T(128)S(1)}, /*index=5*/s32[]{:T(128)}, s32[]{:T(128)}, s32[]{:T(128)}) while((s32[]{:T(128)}, bf16[2,512,256]{2,1,0:T(8,128)(2,1)S(1)}, bf16[2,512,768]{2,1,0:T(8,128)(2,1)}, ...), condition=%wide.region_7.8_spmd, body=%wide.region_2.7_spmd.sunk | while | flops 137174784 | bytes 10541854 | solution.py:119
  71.4 1.3 constant_dynamic-slice_fusion.4
  73.4 0.6 dynamic_slice.70
  74.0 0.7 broadcast_compare_fusion.3
  74.7 2.7 while.45
  76.9 0.4 fusion.125
  77.9 1.2 constant_dynamic-slice_fusion.4
  79.7 0.6 dynamic_slice.70
  80.3 0.7 broadcast_compare_fusion.3
  81.0 2.7 while.45
  81.9 0.4 fusion.125
  83.2 0.4 fusion.125
  84.3 13.0 %all_to_all.20 = bf16[8,64,2,1,256]{4,1,2,3,0:T(8,128)(2,1)S(1)} all-to-all(bf16[8,64,2,1,256]{4,1,2,3,0:T(8,128)(2,1)S(1)} %fusion.65), channel_id=1, replica_groups=mesh['frame'=4,'space'=8] {'space'}, dimensions={0} | all-to-all | bytes 1048576 | tf_op jit(solution)/shard_map/all_to_all | solution.py:125
  97.3 0.5 copy.70
  98.0 42.2 %all-gather.7.cloned.1.call-done = bf16[2048,3072]{1,0:T(8,128)(2,1)} async-done(((bf16[256,3072]{1,0:T(8,128)(2,1)}), bf16[2048,3072]{1,0:T(8,128)(2,1)}) %all-gather.7.cloned.1.call-update) | async-done | bytes 12582928 | tf_op jit(solution)/shard_map/all_gather | solution.py:123
  140.3 7.7 %convert_reduce_fusion = f32[128,3072]{1,0:T(8,128)} fusion(bf16[128,8,256]{2,0,1:T(8,128)(2,1)S(1)} %reshape_reshape_reshape.3, bf16[8,256,3072]{2,1,0:T(8,128)(2,1)} %bitcast.180), kind=kOutput, calls=%fused_computation.53 | convolution fusion | flops 1619656704 | bytes 14680064 | tf_op jit(solution)/shard_map/rgc,gcd->rgd/dot_general | solution.py:89
  147.9 2.2 reshape.318
  150.2 0.7 convert_reduce_fusion.2
  151.2 1.3 fusion.58
  152.6 0.5 all-gather.11.cloned.1.call-update
  153.1 6.7 %slice_bitcast_fusion.2 = (bf16[3072,512]{1,0:T(8,128)(2,1)}, bf16[3072,512]{1,0:T(8,128)(2,1)}, bf16[3072,512]{1,0:T(8,128)(2,1)}) fusion(bf16[3,3072,512]{2,1,0:T(8,128)(2,1)} %param.24), kind=kLoop, calls=%fused_computation.72 | loop fusion | bytes 18874368 | tf_op jit(solution)/shard_map/squeeze | solution.py:143
  159.9 54.6 %all-gather.9.cloned.1.call-done = bf16[2,4,64,3072]{3,2,0,1:T(8,128)(2,1)} async-done(((bf16[2,1,64,3072]{3,2,0,1:T(8,128)(2,1)}), bf16[2,4,64,3072]{3,2,0,1:T(8,128)(2,1)}) %all-gather.9.cloned.1.call-update) | async-done | bytes 3145744 | tf_op jit(solution)/shard_map/all_gather | solution.py:145
  214.5 9.7 %fusion.45 = bf16[2,4,64,1536]{3,2,1,0:T(8,128)(2,1)S(1)} fusion(bf16[3072,512]{1,0:T(8,128)(2,1)} %get-tuple-element.248, bf16[3072,512]{1,0:T(8,128)(2,1)} %get-tuple-element.249, bf16[3072,512]{1,0:T(8,128)(2,1)} %get-tuple-element.247, bf16[2,4,64,3072]{3,2,0,1:T(8,128)(2,1)} %all-gather.9.cloned.1.call-done), kind=kOutput, calls=%fused_computation.73 | convolution fusion | flops 4860936192 | bytes 14155776 | tf_op jit(solution)/shard_map/dot_general | solution.py:144
  224.1 11.9 %while.44 = (s32[]{:T(128)}, bf16[2,4,64,512]{3,2,0,1:T(8,128)(2,1)}, bf16[2,4,64,1536]{3,2,1,0:T(8,128)(2,1)S(1)}, s32[2]{0:T(128)S(1)}, s32[]{:T(128)}) while((s32[]{:T(128)}, bf16[2,4,64,512]{3,2,0,1:T(8,128)(2,1)}, bf16[2,4,64,1536]{3,2,1,0:T(8,128)(2,1)S(1)}, s32[2]{0:T(128)S(1)}, s32[]{:T(128)}) %tuple.106), condition=%wide.region_14.15_spmd, body=%wide.region_11.14_spmd.sunk | while | flops 2252841 | bytes 7479929 | solution.py:154
  224.4 0.8 reshape.328
  225.1 1.4 fusion.117
  226.9 0.6 dynamic_slice.72
  227.5 0.7 iota_compare_fusion.3
  229.4 0.7 bitcast_dynamic-update-slice_fusion.2
  230.3 0.8 reshape.328
  231.1 1.4 fusion.117
  232.8 0.6 dynamic_slice.72
  233.4 0.7 iota_compare_fusion.3
  235.3 0.7 bitcast_dynamic-update-slice_fusion.2
  236.0 6.2 %all-to-all-start.1 = ((bf16[4,2,64,512]{3,2,1,0:T(8,128)(2,1)}), bf16[4,2,64,512]{3,2,1,0:T(8,128)(2,1)S(1)}, u32[]{:S(2)}, u32[]{:S(2)}) async-start(bf16[4,2,64,512]{3,2,1,0:T(8,128)(2,1)} %bitcast.196), calls=%async_computation.1 | async-start | bytes 1048576 | tf_op jit(solution)/shard_map/all_to_all | solution.py:157
  242.3 0.6 multiply_reduce_fusion.1
  243.6 198.7 %all-gather.11.cloned.1.call-done = bf16[2048,3072]{1,0:T(8,128)(2,1)} async-done(((bf16[512,3072]{1,0:T(8,128)(2,1)}), bf16[2048,3072]{1,0:T(8,128)(2,1)}) %all-gather.11.cloned.1.call-update) | async-done | bytes 12582928 | tf_op jit(solution)/shard_map/all_gather | solution.py:156
  442.2 6.6 %convert_reduce_fusion.1 = f32[128,3072]{1,0:T(8,128)S(1)} fusion(bf16[128,4,512]{2,0,1:T(8,128)(2,1)S(1)} %bitcast.185, bf16[4,512,3072]{2,1,0:T(8,128)(2,1)} %bitcast.181), kind=kOutput, calls=%fused_computation.62 | convolution fusion | flops 1614938112 | bytes 14680064 | tf_op jit(solution)/shard_map/rgc,gcd->rgd/dot_general | solution.py:89
  448.9 1.4 multiply_reduce_fusion
  450.2 0.7 fusion.75
  450.9 44.4 %psum.7 = f32[]{:T(128)} all-reduce(f32[]{:T(128)} %fusion.75), channel_id=1, replica_groups=mesh['frame'=4,'space'=8] {'frame','space'}, use_global_device_ids=true, to_apply=%region_18.19 | all-reduce | flops 1 | bytes 8 | tf_op jit(solution)/shard_map/psum | solution.py:172
  (100 shorter events, 11.2 us)
Async XLA Ops:
  7.2 54.4 %all-gather.5.cloned.1.call-start = ((), (), s32[]{:S(2)}) async-start(), calls=%async_computation.2 | async-start | bytes 7077888 | tf_op jit(solution)/shard_map/all_gather | solution.py:106
  8.0 5.1 %copy-start = (bf16[2,1,64,3072]{3,2,1,0:T(8,128)(2,1)S(1)}, bf16[2,1,64,3072]{3,2,1,0:T(8,128)(2,1)}, u32[]{:S(2)}) copy-start(bf16[2,1,64,3072]{3,2,1,0:T(8,128)(2,1)} %param.16) | copy-start | bytes 2359300
  15.0 0.8 copy-start.3
  15.0 125.2 %all-gather.7.cloned.1.call-start = ((), (), s32[]{:S(2)}) async-start(), calls=%async_computation.3 | async-start | bytes 14155776 | tf_op jit(solution)/shard_map/all_gather | solution.py:123
  15.8 198.7 %all-gather.9.cloned.1.call-start = ((), (), s32[]{:S(2)}) async-start(), calls=%async_computation.4 | async-start | bytes 3932160 | tf_op jit(solution)/shard_map/all_gather | solution.py:145
  61.6 9.9 %copy-start.2 = (s32[2,16,16]{2,1,0:T(8,128)S(1)}, s32[2,16,16]{2,1,0:T(8,128)}, u32[]{:S(2)}) copy-start(s32[2,16,16]{2,1,0:T(8,128)} %param.20) | copy-start | bytes 6148
  152.6 289.7 %all-gather.11.cloned.1.call-start = ((), (), s32[]{:S(2)}) async-start(), calls=%async_computation.5 | async-start | bytes 15728640 | tf_op jit(solution)/shard_map/all_gather | solution.py:156
  236.0 206.2 %all-to-all-start.1 = ((bf16[4,2,64,512]{3,2,1,0:T(8,128)(2,1)}), bf16[4,2,64,512]{3,2,1,0:T(8,128)(2,1)S(1)}, u32[]{:S(2)}, u32[]{:S(2)}) async-start(bf16[4,2,64,512]{3,2,1,0:T(8,128)(2,1)} %bitcast.196), calls=%async_computation.1 | async-start | bytes 1048576 | tf_op jit(solution)/shard_map/all_to_all | solution.py:157
  442.2 6.6 %copy-start.1 = (bf16[2,1,64,3072]{3,2,1,0:T(8,128)(2,1)S(1)}, bf16[2,1,64,3072]{3,2,1,0:T(8,128)(2,1)}, u32[]{:S(2)}) copy-start(bf16[2,1,64,3072]{3,2,1,0:T(8,128)(2,1)} %param.17) | copy-start | bytes 2359300
Sparse Core Ops, SparseCore 0:
  15.1 46.3 all-gather.4
  63.5 76.7 all-gather.6
  152.7 61.7 all-gather.8
  215.9 226.3 all-gather.10
